TPU v7x, 32 devices: a whole 2x2x4 slice. The times are simulated.
32 devices in a mesh: wide: 8 (over y, x, core), narrow: 4 (over z).
Axes of the slice: x: 2, y: 2, z: 4, core: 2. Of those that a mesh axis runs over, the one named last changes fastest.
Arguments:
- tokens: bfloat16 [16384, 768], P(('wide', 'narrow')), may hold values from -6 to 6
- noise: int32 [16384], P(('wide', 'narrow')), may hold values 0 or 1
- seq_lengths: int32 [8, 4], P('wide'), may hold values from 0 to 2048, as said below
- ln1_gain: float32 [768], replicated, may hold values from 0.25 to 1.75
- ln1_bias: float32 [768], replicated, may hold values from -3 to 3
- qkv_weight: bfloat16 [3, 768, 768], P(None, None, 'narrow'), may hold values from -0.21875 to 0.21875
- out_weight: bfloat16 [768, 768], P('narrow'), may hold values from -3 to 3
- ln2_gain: float32 [768], replicated, may hold values from 0.25 to 1.75
- ln2_bias: float32 [768], replicated, may hold values from -3 to 3
- up_weight: bfloat16 [768, 3072], P(None, 'narrow'), may hold values from -0.21875 to 0.21875
- up_bias: float32 [3072], P('narrow'), may hold values from -4 to 4
- down_weight: bfloat16 [3072, 768], P('narrow'), may hold values from -0.109375 to 0.109375
- down_bias: float32 [768], replicated, may hold values from -3 to 3
- mask_vector: float32 [768], replicated, may hold values from -4 to 4
- cotangent: bfloat16 [2, 16384, 768], P(None, ('wide', 'narrow')), may hold values from -6 to 6
Outputs:
- output: bfloat16 [2, 16384, 768], P(None, ('wide', 'narrow'))
- d_tokens: bfloat16 [16384, 768], P(('wide', 'narrow'))
- d_ln1_gain: float32 [768], replicated
- d_ln1_bias: float32 [768], replicated
- d_qkv_weight: float32 [3, 768, 768], P(None, 'wide', 'narrow')
- d_out_weight: float32 [768, 768], P('narrow', 'wide')
- d_ln2_gain: float32 [768], replicated
- d_ln2_bias: float32 [768], replicated
- d_up_weight: float32 [768, 3072], P('wide', 'narrow')
- d_up_bias: float32 [3072], P(('narrow', 'wide'))
- d_down_weight: float32 [3072, 768], P('narrow', 'wide')
- d_down_bias: float32 [768], replicated
- d_mask_vector: float32 [768], replicated
Inputs may be any that keep to these rules, and one draw needn't show every extreme that they name: `seq_lengths`: row w lists the sequences packed on index w of wide in order; every length is a multiple of 16 and a row sums to 2048. A quarter of the rows hold one sequence of 2048 tokens followed by zeros; the others hold four sequences, each at least 1 token long.
All inputs are finite; a program needn't handle non-finite values. No bound on the sum of `noise` on one device may be relied on, other than what follows from the above.
Results may differ from a plain program's by a relative error of at most 0.019.
Values may be sent and summed in bfloat16 or wider, within the bound.
No kernel may reach another device: no remote copies, remote signals or barrier semaphores. Data moves between devices by JAX's collectives and lax.ppermute only.
A program may use at most 256 MiB of HBM per device.

v0:
```python
import math

import jax
import jax.numpy as jnp
from jax import lax
from jax.sharding import PartitionSpec as P

HEAD = 64
BLOCK = 16


EPS = 1e-05


def layer_norm(values, gain, shift):
    center = values - jnp.mean(values, axis=-1, keepdims=True)
    spread = jnp.mean(center * center, axis=-1, keepdims=True)
    return center * lax.rsqrt(spread + EPS) * gain + shift


def gelu_tanh(values):
    return jax.nn.gelu(values, approximate=True)


def rotate(values, cosines, sines):
    half = values.shape[-1] // 2
    turned = jnp.concatenate([-values[..., half:], values[..., :half]], axis=-1)
    return values * cosines + turned * sines


def angle_tables(positions, head):
    index_f = jnp.arange(head // 2).astype(jnp.float32)
    freqs = jnp.exp(index_f * (-2.0 * math.log(10000.0) / head))
    angles = positions.astype(jnp.float32)[:, None] * freqs[None, :]
    cosines = jnp.concatenate([jnp.cos(angles), jnp.cos(angles)], axis=-1)[:, None, :]
    sines = jnp.concatenate([jnp.sin(angles), jnp.sin(angles)], axis=-1)[:, None, :]
    return (cosines, sines)


def token_meta(lengths_row, count, block):
    ends = jnp.cumsum(lengths_row)
    starts = ends - lengths_row
    places = jnp.arange(count)
    seq_id = jnp.sum((places[:, None] >= ends[None, :]).astype(jnp.int32), axis=1)
    slot_ids = jnp.arange(lengths_row.shape[0])
    first = jnp.sum(jnp.where(seq_id[:, None] == slot_ids[None, :], starts[None, :], 0), axis=1)
    return (seq_id, places - first, places // block)


def allowed_pairs(q_seq, q_blk, q_copy, k_seq, k_blk, k_copy):
    same = q_seq[:, None] == k_seq[None, :]
    q_b = q_blk[:, None]
    k_b = k_blk[None, :]
    q_noisy = q_copy[:, None] == 0
    k_noisy = k_copy[None, :] == 0
    rule = jnp.where(
        q_noisy,
        jnp.where(k_noisy, q_b == k_b, k_b < q_b),
        jnp.logical_and(jnp.logical_not(k_noisy), k_b <= q_b),
    )
    return jnp.logical_and(same, rule)


def inner_rows(left, right):
    return lax.dot_general(
        left, right, (((0,), (0,)), ((), ())), preferred_element_type=jnp.float32
    )


def times_trans(left, right):
    return lax.dot_general(
        left, right, (((1,), (1,)), ((), ())), preferred_element_type=jnp.float32
    )


def per_device(
    tokens,
    noise,
    seq_lengths,
    ln1_gain,
    ln1_bias,
    qkv_weight,
    out_weight,
    ln2_gain,
    ln2_bias,
    up_weight,
    up_bias,
    down_weight,
    down_bias,
    mask_vector,
    cotangent,
):
    f32 = jnp.float32
    bf16 = jnp.bfloat16
    rows_dev, width = tokens.shape
    group_rows = rows_dev * lax.axis_size("narrow")
    count = 2 * group_rows
    local_width = qkv_weight.shape[2]
    heads_dev = local_width // HEAD
    scale = 1.0 / math.sqrt(HEAD)
    width_q = min(512, count)
    count_b = count // width_q
    clean = tokens.astype(f32)
    noisy = jnp.where(noise[:, None] == 1, mask_vector[None, :], clean)
    resid = jnp.stack([noisy, clean])
    normed1, norm1_pull = jax.vjp(layer_norm, resid, ln1_gain, ln1_bias)
    a_all = lax.all_gather(normed1.astype(bf16), "narrow", axis=1, tiled=True).reshape(count, width)
    seq_id, pos, blk = token_meta(seq_lengths[0], group_rows, BLOCK)
    seq2 = jnp.concatenate([seq_id, seq_id])
    pos2 = jnp.concatenate([pos, pos])
    blk2 = jnp.concatenate([blk, blk])
    copy2 = jnp.concatenate(
        [jnp.zeros((group_rows,), jnp.int32), jnp.ones((group_rows,), jnp.int32)]
    )
    cosines, sines = angle_tables(pos2, HEAD)

    def turn(values):
        return rotate(values, cosines, sines)

    q_pre = jnp.dot(a_all, qkv_weight[0], preferred_element_type=f32).reshape(
        count, heads_dev, HEAD
    )
    k_pre = jnp.dot(a_all, qkv_weight[1], preferred_element_type=f32).reshape(
        count, heads_dev, HEAD
    )
    q_rot, q_pull = jax.vjp(turn, q_pre)
    k_rot, k_pull = jax.vjp(turn, k_pre)
    queries = q_rot.astype(bf16)
    keys = k_rot.astype(bf16)
    values = (
        jnp.dot(a_all, qkv_weight[2], preferred_element_type=f32)
        .astype(bf16)
        .reshape(count, heads_dev, HEAD)
    )
    query_blocks = queries.reshape(count_b, width_q, heads_dev, HEAD)
    seq_blocks = seq2.reshape(count_b, width_q)
    blk_blocks = blk2.reshape(count_b, width_q)
    copy_blocks = copy2.reshape(count_b, width_q)

    def forward_block(item):
        q_block, q_seq, q_blk, q_copy = item
        scores = jnp.einsum("qhd,khd->hqk", q_block, keys, preferred_element_type=f32) * scale
        mask = allowed_pairs(q_seq, q_blk, q_copy, seq2, blk2, copy2)
        scores = jnp.where(mask[None], scores, -1e30)
        top = jnp.max(scores, axis=2, keepdims=True)
        lse = top + jnp.log(jnp.sum(jnp.exp(scores - top), axis=2, keepdims=True))
        probs = jnp.exp(scores - lse).astype(bf16)
        return (jnp.einsum("hqk,khd->qhd", probs, values, preferred_element_type=f32), lse[:, :, 0])

    attn_blocks, lse_blocks = lax.map(
        forward_block, (query_blocks, seq_blocks, blk_blocks, copy_blocks)
    )
    attn = attn_blocks.reshape(count, local_width).astype(bf16)
    attn_part = jnp.dot(attn, out_weight, preferred_element_type=f32).reshape(2, group_rows, width)
    attn_out = lax.psum_scatter(
        attn_part.astype(jnp.bfloat16), "narrow", scatter_dimension=1, tiled=True
    ).astype(jnp.float32)
    h_mid = resid + attn_out
    normed2, norm2_pull = jax.vjp(layer_norm, h_mid, ln2_gain, ln2_bias)
    b_all = lax.all_gather(normed2.astype(bf16), "narrow", axis=1, tiled=True).reshape(count, width)
    up_pre = jnp.dot(b_all, up_weight, preferred_element_type=f32) + up_bias
    hidden_f, gelu_pull = jax.vjp(gelu_tanh, up_pre)
    hidden = hidden_f.astype(bf16)
    down_part = jnp.dot(hidden, down_weight, preferred_element_type=f32).reshape(
        2, group_rows, width
    )
    mlp_out = lax.psum_scatter(
        down_part.astype(jnp.bfloat16), "narrow", scatter_dimension=1, tiled=True
    ).astype(jnp.float32)
    output = (h_mid + mlp_out + down_bias).astype(bf16)
    grad_out = cotangent.astype(f32)
    d_down_bias = jnp.sum(grad_out, axis=(0, 1))
    cot_all = lax.all_gather(cotangent, "narrow", axis=1, tiled=True).reshape(count, width)
    d_down = inner_rows(hidden, cot_all)
    d_hidden = times_trans(cot_all, down_weight)
    d_up_low = gelu_pull(d_hidden)[0].astype(bf16)
    d_up = inner_rows(b_all, d_up_low)
    d_up_bias = jnp.sum(d_up_low, axis=0, dtype=f32)
    d_b_part = times_trans(d_up_low, up_weight).reshape(2, group_rows, width)
    d_normed2 = lax.psum_scatter(
        d_b_part.astype(jnp.bfloat16), "narrow", scatter_dimension=1, tiled=True
    ).astype(jnp.float32)
    d_h_ln, d_ln2_gain, d_ln2_bias = norm2_pull(d_normed2)
    d_h_mid = grad_out + d_h_ln
    d_z = d_h_mid.astype(bf16)
    d_z_all = lax.all_gather(d_z, "narrow", axis=1, tiled=True).reshape(count, width)
    d_out = inner_rows(attn, d_z_all)
    d_attn = times_trans(d_z_all, out_weight).astype(bf16)
    d_attn_blocks = d_attn.reshape(count_b, width_q, heads_dev, HEAD)

    def backward_block(carry, item):
        d_keys, d_values = carry
        q_block, lse_block, d_block, q_seq, q_blk, q_copy = item
        scores = jnp.einsum("qhd,khd->hqk", q_block, keys, preferred_element_type=f32) * scale
        mask = allowed_pairs(q_seq, q_blk, q_copy, seq2, blk2, copy2)
        scores = jnp.where(mask[None], scores, -1e30)
        probs = jnp.exp(scores - lse_block[:, :, None])
        d_probs = jnp.einsum("qhd,khd->hqk", d_block, values, preferred_element_type=f32)
        delta = jnp.sum(d_probs * probs, axis=2, keepdims=True)
        d_scores = (probs * (d_probs - delta)).astype(bf16)
        d_query = jnp.einsum("hqk,khd->qhd", d_scores, keys, preferred_element_type=f32) * scale
        d_keys = (
            d_keys
            + jnp.einsum("hqk,qhd->khd", d_scores, q_block, preferred_element_type=f32) * scale
        )
        d_values = d_values + jnp.einsum(
            "hqk,qhd->khd", probs.astype(bf16), d_block, preferred_element_type=f32
        )
        return ((d_keys, d_values), d_query)

    empty = jnp.zeros((count, heads_dev, HEAD), f32)
    (d_keys, d_values), d_query_blocks = lax.scan(
        backward_block,
        (empty, empty),
        (query_blocks, lse_blocks, d_attn_blocks, seq_blocks, blk_blocks, copy_blocks),
    )
    d_q_low = (
        q_pull(d_query_blocks.reshape(count, heads_dev, HEAD))[0]
        .astype(bf16)
        .reshape(count, local_width)
    )
    d_k_low = k_pull(d_keys)[0].astype(bf16).reshape(count, local_width)
    d_v_low = d_values.astype(bf16).reshape(count, local_width)
    d_qkv = jnp.stack(
        [inner_rows(a_all, d_q_low), inner_rows(a_all, d_k_low), inner_rows(a_all, d_v_low)]
    )
    d_a_part = (
        times_trans(d_q_low, qkv_weight[0])
        + times_trans(d_k_low, qkv_weight[1])
        + times_trans(d_v_low, qkv_weight[2])
    ).reshape(2, group_rows, width)
    d_normed1 = lax.psum_scatter(
        d_a_part.astype(jnp.bfloat16), "narrow", scatter_dimension=1, tiled=True
    ).astype(jnp.float32)
    d_resid_ln, d_ln1_gain, d_ln1_bias = norm1_pull(d_normed1)
    d_resid = d_h_mid + d_resid_ln
    masked = noise[:, None] == 1
    d_tokens = (d_resid[1] + jnp.where(masked, 0.0, d_resid[0])).astype(bf16)
    d_mask = jnp.sum(jnp.where(masked, d_resid[0], 0.0), axis=0)
    summed = (
        lax.psum_scatter(d_qkv, "wide", scatter_dimension=1, tiled=True),
        lax.psum_scatter(d_out, "wide", scatter_dimension=1, tiled=True),
        lax.psum_scatter(d_up, "wide", scatter_dimension=0, tiled=True),
        lax.psum_scatter(d_down, "wide", scatter_dimension=1, tiled=True),
        lax.psum_scatter(d_up_bias[None, :], "wide", scatter_dimension=1, tiled=True),
    )
    small = lax.psum(
        (d_ln1_gain, d_ln1_bias, d_ln2_gain, d_ln2_bias, d_down_bias, d_mask), ("wide", "narrow")
    )
    return (
        output,
        d_tokens,
        small[0],
        small[1],
        summed[0],
        summed[1],
        small[2],
        small[3],
        summed[2],
        summed[4][0],
        summed[3],
        small[4],
        small[5],
    )


def solution(mesh):
    placed = (
        P(("wide", "narrow"), None),
        P(("wide", "narrow")),
        P("wide", None),
        P(),
        P(),
        P(None, None, "narrow"),
        P("narrow", None),
        P(),
        P(),
        P(None, "narrow"),
        P("narrow"),
        P("narrow", None),
        P(),
        P(),
        P(None, ("wide", "narrow"), None),
    )
    return jax.shard_map(
        per_device,
        mesh=mesh,
        in_specs=placed,
        out_specs=(
            P(None, ("wide", "narrow"), None),
            P(("wide", "narrow"), None),
            P(),
            P(),
            P(None, "wide", "narrow"),
            P("narrow", "wide"),
            P(),
            P(),
            P("wide", "narrow"),
            P(("narrow", "wide")),
            P("narrow", "wide"),
            P(),
            P(),
        ),
        check_vma=False,
    )
```

profile of v0, /device:TPU:0, one launch (start us, length us, event | category | flops | bytes accessed | tf_op | source)
XLA Modules:
  0.0 2366.9 jit_solution(2762413686105143079)
XLA Ops:
  20.2 113.0 %all-gather.5.cloned.1.call-done = bf16[2,2048,768]{2,1,0:T(8,128)(2,1)} async-done(((bf16[2,512,768]{2,1,0:T(8,128)(2,1)}), bf16[2,2048,768]{2,1,0:T(8,128)(2,1)}) %all-gather.5.cloned.1.call-update) | async-done | bytes 6291472 | tf_op jit(solution)/shard_map/all_gather | solution.py:107
  148.6 346.6 %while.27 = (s32[]{:T(128)}, bf16[8,512,3,64]{1,3,2,0:T(8,128)(2,1)}, f32[8,3,512]{2,1,0:T(4,128)}, s32[8,512]{1,0:T(8,128)}, s32[4096]{0:T(1024)S(1)}, /*index=...) while((s32[]{:T(128)}, ...), condition=%wide.region_8.9_spmd, body=%wide.region_5.8_spmd.sunk | while | flops 1696594944 | bytes 94020792 | solution.py:150
  508.9 109.1 %reduce-scatter.16.cloned.1.call-done = bf16[2,512,768]{2,1,0:T(8,128)(2,1)} async-done(((bf16[2,2048,768]{2,1,0:T(8,128)(2,1)}), bf16[2,512,768]{2,1,0:T(8,128)(2,1)}) %reduce-scatter.16.cloned.1.call-update) | async-done | bytes 1572880 | tf_op jit(solution)/shard_map/reduce_scatter | solution.py:155
  624.9 115.4 %all-gather.7.cloned.1.call-done = bf16[2,2048,768]{2,1,0:T(8,128)(2,1)} async-done(((bf16[2,512,768]{2,1,0:T(8,128)(2,1)}), bf16[2,2048,768]{2,1,0:T(8,128)(2,1)}) %all-gather.7.cloned.1.call-update) | async-done | bytes 6291472 | tf_op jit(solution)/shard_map/all_gather | solution.py:160
  750.8 104.4 %all-gather.9.cloned.1.call-done = bf16[2,2048,768]{2,1,0:T(8,128)(2,1)} async-done(((bf16[2,512,768]{2,1,0:T(8,128)(2,1)}), bf16[2,2048,768]{2,1,0:T(8,128)(2,1)}) %all-gather.9.cloned.1.call-update) | async-done | bytes 6291472 | tf_op jit(solution)/shard_map/all_gather | solution.py:173
  855.2 18.5 convert_reduce_fusion
  880.8 109.1 %reduce-scatter.20.cloned.1.call-done = bf16[2,512,768]{2,1,0:T(8,128)(2,1)} async-done(((bf16[2,2048,768]{2,1,0:T(8,128)(2,1)}), bf16[2,512,768]{2,1,0:T(8,128)(2,1)}) %reduce-scatter.20.cloned.1.call-update) | async-done | bytes 1572880 | tf_op jit(solution)/shard_map/reduce_scatter | solution.py:180
  1003.5 111.3 %all-gather.11.cloned.1.call-done = bf16[2,2048,768]{2,1,0:T(8,128)(2,1)} async-done(((bf16[2,512,768]{2,1,0:T(8,128)(2,1)}), bf16[2,2048,768]{2,1,0:T(8,128)(2,1)}) %all-gather.11.cloned.1.call-update) | async-done | bytes 6291472 | tf_op jit(solution)/shard_map/all_gather | solution.py:186
  1128.3 818.9 %while.28 = (s32[]{:T(128)}, f32[4096,3,64]{0,2,1:T(8,128)}, f32[4096,3,64]{0,2,1:T(8,128)}, f32[8,512,3,64]{1,0,3,2:T(8,128)}, bf16[8,512,3,64]{1,3,2,0:T(8,128...) while((s32[]{:T(128)}, f32[4096,3,64]{0,2,1:T(8,128)}, ...), condition=%wide.region_18.19_spmd.clone, body=%wide.region_16.18_spmd.clone.sunk | while | flops 4141710336 | bytes 229868800 | solution.py:212
  1180.6 21.7 multiply_convert_fusion.3
  1282.2 21.7 multiply_convert_fusion.3
  1384.6 21.7 multiply_convert_fusion.3
  1487.1 21.7 multiply_convert_fusion.3
  1571.4 18.2 multiply_reduce_fusion.4
  1589.6 21.7 multiply_convert_fusion.3
  1692.1 21.7 multiply_convert_fusion.3
  1776.4 18.2 multiply_reduce_fusion.4
  1794.6 21.7 multiply_convert_fusion.3
  1878.9 18.2 multiply_reduce_fusion.4
  1897.1 21.7 multiply_convert_fusion.3
  2050.2 103.0 %reduce-scatter.22.cloned.1.call-done = bf16[2,512,768]{2,1,0:T(8,128)(2,1)} async-done(((bf16[2,2048,768]{2,1,0:T(8,128)(2,1)}), bf16[2,512,768]{2,1,0:T(8,128)(2,1)}) %reduce-scatter.22.cloned.1.call-update) | async-done | bytes 1572880 | tf_op jit(solution)/shard_map/reduce_scatter | solution.py:232
  2158.3 108.6 %reduce-scatter.18.cloned.1.call-done = bf16[2,512,768]{2,1,0:T(8,128)(2,1)} async-done(((bf16[2,2048,768]{2,1,0:T(8,128)(2,1)}), bf16[2,512,768]{2,1,0:T(8,128)(2,1)}) %reduce-scatter.18.cloned.1.call-update) | async-done | bytes 1572880 | tf_op jit(solution)/shard_map/reduce_scatter | solution.py:167
  2275.0 41.5 %all-reduce.4 = (f32[768]{0:T(1024)}, f32[768]{0:T(1024)}, f32[768]{0:T(1024)}, f32[768]{0:T(1024)}, f32[768]{0:T(1024)}, /*index=5*/f32[768]{0:T(1024)}) all-reduce(f32[768]{0:T(1024)S(1)} %get-tuple-element.328, f32[768]{0:T(1024)S(1)} %get-tuple-element.332, ...), channel_id=1, replica_groups=mesh['wide'=8,'narrow'=4] {'wide','narrow'}, use_global_device_ids=true, to_apply=%region_23.24 | all-reduce | flops 4608 | bytes 36864 | tf_op jit(solution)/shard_map/psum | solution.py:247
  2316.5 43.7 %reduce-scatter.26.cloned.1.call-done = f32[768,96]{0,1:T(8,128)} async-done(((f32[768,768]{0,1:T(8,128)}), f32[768,96]{0,1:T(8,128)}) %reduce-scatter.26.cloned.1.call-update) | async-done | bytes 294928 | tf_op jit(solution)/shard_map/reduce_scatter | solution.py:244
  (417 shorter events, 1145.2 us)
Async XLA Ops:
  7.2 848.0 %copy-start = (bf16[768,768]{1,0:T(8,128)(2,1)S(1)}, bf16[768,768]{1,0:T(8,128)(2,1)}, u32[]{:S(2)}) copy-start(bf16[768,768]{1,0:T(8,128)(2,1)} %param.30) | copy-start | bytes 3538948
  7.2 126.0 %all-gather.5.cloned.1.call-start = ((), (), s32[]{:S(2)}) async-start(), calls=%async_computation.9 | async-start | bytes 7864320 | tf_op jit(solution)/shard_map/all_gather | solution.py:107
  15.0 603.0 %reduce-scatter.16.cloned.1.call-start = ((), (), s32[]{:S(2)}) async-start(), calls=%async_computation.10 | async-start | bytes 7864320 | tf_op jit(solution)/shard_map/reduce_scatter | solution.py:155
  508.8 231.4 %all-gather.7.cloned.1.call-start = ((), (), s32[]{:S(2)}) async-start(), calls=%async_computation.11 | async-start | bytes 7864320 | tf_op jit(solution)/shard_map/all_gather | solution.py:160
  620.7 375.8 %copy-start.27 = (f32[2,512]{1,0:T(2,128)}, f32[2,512]{1,0:T(2,128)S(1)}, u32[]{:S(2)}) copy-start(f32[2,512]{1,0:T(2,128)S(1)} %broadcast_multiply_fusion.2) | copy-start | bytes 12292
  622.5 374.0 %copy-start.33 = (f32[2,512]{1,0:T(2,128)}, f32[2,512]{1,0:T(2,128)S(1)}, u32[]{:S(2)}) copy-start(f32[2,512]{1,0:T(2,128)S(1)} %fusion.81) | copy-start | bytes 12292
  624.2 231.0 %all-gather.9.cloned.1.call-start = ((), (), s32[]{:S(2)}) async-start(), calls=%async_computation.13 | async-start | bytes 7864320 | tf_op jit(solution)/shard_map/all_gather | solution.py:173
  624.8 365.1 %reduce-scatter.20.cloned.1.call-start = ((), (), s32[]{:S(2)}) async-start(), calls=%async_computation.14 | async-start | bytes 7864320 | tf_op jit(solution)/shard_map/reduce_scatter | solution.py:180
  740.2 115.0 %copy-start.55 = (f32[768]{0:T(1024)S(1)}, f32[768]{0:T(1024)}, u32[]{:S(2)}) copy-start(f32[768]{0:T(1024)} %param.29) | copy-start | bytes 9220
  880.8 234.0 %all-gather.11.cloned.1.call-start = ((), (), s32[]{:S(2)}) async-start(), calls=%async_computation.15 | async-start | bytes 7864320 | tf_op jit(solution)/shard_map/all_gather | solution.py:186
  998.8 1046.3 %reduce-scatter.32.cloned.1.call-start = ((), (), s32[]{:S(2)}) async-start(), calls=%async_computation.21 | async-start | bytes 442368
  1003.4 1043.1 %reduce-scatter.30.cloned.1.call-start = ((), (), s32[]{:S(2)}) async-start(), calls=%async_computation.20 | async-start | bytes 884736
  1963.4 84.8 %reduce-scatter.28.cloned.1.call-start = ((), (), s32[]{:S(2)}) async-start(), calls=%async_computation.19 | async-start | bytes 2211840
  1986.4 166.9 %reduce-scatter.22.cloned.1.call-start = ((), (), s32[]{:S(2)}) async-start(), calls=%async_computation.16 | async-start | bytes 7864320 | tf_op jit(solution)/shard_map/reduce_scatter | solution.py:232
  2014.6 252.3 %reduce-scatter.18.cloned.1.call-start = ((), (), s32[]{:S(2)}) async-start(), calls=%async_computation.12 | async-start | bytes 7864320 | tf_op jit(solution)/shard_map/reduce_scatter | solution.py:167
  2024.3 292.1 %reduce-scatter.24.cloned.1.call-start = ((), (), s32[]{:S(2)}) async-start(), calls=%async_computation.17 | async-start | bytes 2654208 | tf_op jit(solution)/shard_map/reduce_scatter | solution.py:243
  2034.6 325.5 %reduce-scatter.26.cloned.1.call-start = ((), (), s32[]{:S(2)}) async-start(), calls=%async_computation.18 | async-start | bytes 2654208 | tf_op jit(solution)/shard_map/reduce_scatter | solution.py:244
  2045.1 111.4 %copy-start.44 = (f32[2,512]{1,0:T(2,128)S(1)}, f32[2,512]{1,0:T(2,128)}, u32[]{:S(2)}) copy-start(f32[2,512]{1,0:T(2,128)} %copy-done.43) | copy-start | bytes 12292
  2156.4 110.5 %copy-start.28 = (f32[2,512]{1,0:T(2,128)S(1)}, f32[2,512]{1,0:T(2,128)}, u32[]{:S(2)}) copy-start(f32[2,512]{1,0:T(2,128)} %copy-done.27) | copy-start | bytes 12292
  2156.4 110.5 %copy-start.32 = (f32[768]{0:T(1024)S(1)}, f32[768]{0:T(1024)}, u32[]{:S(2)}) copy-start(f32[768]{0:T(1024)} %param.26) | copy-start | bytes 9220
  2156.4 110.5 %copy-start.34 = (f32[2,512]{1,0:T(2,128)S(1)}, f32[2,512]{1,0:T(2,128)}, u32[]{:S(2)}) copy-start(f32[2,512]{1,0:T(2,128)} %copy-done.33) | copy-start | bytes 12292
  2156.4 110.5 %copy-start.36 = (f32[2,512]{1,0:T(2,128)S(1)}, f32[2,512]{1,0:T(2,128)}, u32[]{:S(2)}) copy-start(f32[2,512]{1,0:T(2,128)} %copy-done.35) | copy-start | bytes 12292
  2156.4 110.5 %copy-start.42 = (f32[2,512]{1,0:T(2,128)S(1)}, f32[2,512]{1,0:T(2,128)}, u32[]{:S(2)}) copy-start(f32[2,512]{1,0:T(2,128)} %copy-done.41) | copy-start | bytes 12292
  2158.3 115.5 %copy-start.48 = (pred[512]{0:T(512)(128)(4,1)S(1)}, pred[512]{0:T(512)(128)(4,1)}, u32[]{:S(2)}) copy-start(pred[512]{0:T(512)(128)(4,1)} %copy-done.47) | copy-start | bytes 1540
  (70 other events, 978.9 us)
Sparse Core Ops, SparseCore 0:
  15.1 118.0 all-gather.4
  509.0 108.9 reduce-scatter.15
  624.4 115.8 all-gather.6
  741.7 113.5 all-gather.8
  880.9 108.9 reduce-scatter.19
  998.9 115.8 all-gather.10
  1117.8 32.0 reduce-scatter.31
  1963.5 33.0 reduce-scatter.29
  2000.1 40.1 reduce-scatter.27
  2042.5 110.7 reduce-scatter.21
  2155.6 111.2 reduce-scatter.17
  2270.7 42.9 reduce-scatter.23
  2317.6 42.4 reduce-scatter.25
where the time goes:
time: 2380 us; the launch traced here: 2370 us
  waiting for transfers between devices  918 us (39%)
  matrix products  833 us (35%)
  other arithmetic  427 us (18%)
  local copies, waits for them, and re-layouts  130 us (5%)
  blocking collectives  41.5 us (2%)
    convert_element_type x8, other arithmetic, backward_block(): d_scores = (probs * (d_probs - delta)).astype(bf16)  174 us
    dot_general x8, matrix products, backward_block(): jnp.einsum('qhd,khd->hqk', d_block, values, preferred_element_type=f32)  146 us
    all_gather x1, waiting for transfers between devices, per_device(): lax.all_gather(normed2.astype(bf16), 'narrow', axis=1, tiled=True)  115 us
    all_gather x1, waiting for transfers between devices, per_device(): lax.all_gather(normed1.astype(bf16), 'narrow', axis=1, tiled=True)  113 us
    all_gather x1, waiting for transfers between devices, per_device(): lax.all_gather(d_z, 'narrow', axis=1, tiled=True).reshape(count, width)  111 us
    dot_general x8, matrix products, backward_block(): jnp.einsum('hqk,qhd->khd', probs.astype(bf16), d_block, preferred_element...  110 us
    reduce_scatter x1, waiting for transfers between devices, per_device(): lax.psum_scatter(attn_part.astype(jnp.bfloat16), 'narrow', scatter_dimens...  109 us
    reduce_scatter x1, waiting for transfers between devices, per_device(): lax.psum_scatter(d_b_part.astype(jnp.bfloat16), 'narrow', scatter_dimensi...  109 us
  transfers between devices with their start and end apart: 13, of which 9 were waited for; matrix products, arithmetic and copies ran while one was open for 41% of the time, Pallas kernels for 0%

commit v1 on v0

v1 whole, which is shorter than its diff:
```python
import math

import jax
import jax.numpy as jnp
from jax import lax
from jax.experimental import pallas as pl
from jax.experimental.pallas import tpu as pltpu
from jax.sharding import PartitionSpec as P

HEAD = 64
BLOCK = 16
EPS = 1e-05


TILE = 256
NEG = -1e30


def nt(left, right):
    return lax.dot_general(
        left, right, (((1,), (1,)), ((), ())), preferred_element_type=jnp.float32
    )


def nn(left, right):
    return lax.dot_general(
        left, right, (((1,), (0,)), ((), ())), preferred_element_type=jnp.float32
    )


def project_kernel(a, amask, masked, w, wrot, cosines, sines, q, k, kt, v, vt):
    rows = a[...]
    spot = amask[...]
    cos = cosines[...]
    sin = sines[...]
    hidden = jnp.broadcast_to(masked[...], cos.shape) == 1
    heads = q.shape[0]

    def both(index, turned):
        pre = nn(rows, w[index])
        pre_m = nn(spot, w[index])[0:1]
        noisy = jnp.where(hidden, pre_m, pre)
        if not turned:
            return noisy, pre
        side = nn(rows, wrot[index])
        side_m = nn(spot, wrot[index])[0:1]
        side_n = jnp.where(hidden, side_m, side)
        return noisy * cos + side_n * sin, pre * cos + side * sin

    for index, (flat, trans) in enumerate(((q, None), (k, kt), (v, vt))):
        pair = both(index, index < 2)
        for copy in range(2):
            low = pair[copy].astype(jnp.bfloat16)
            if index == 0:
                low = low * jnp.asarray(1.0 / math.sqrt(HEAD), jnp.bfloat16)
            for head in range(heads):
                piece = low[:, head * HEAD : (head + 1) * HEAD]
                flat[head, copy] = piece
                if trans is not None:
                    trans[head, copy] = piece.T


def tile_masks(start, base, tile):
    key = lax.broadcasted_iota(jnp.int32, (tile, tile), 0)
    query = lax.broadcasted_iota(jnp.int32, (tile, tile), 1)
    kb = key // BLOCK
    qb = query // BLOCK
    same = key + base >= start
    return kb == qb, jnp.logical_and(kb < qb, same), jnp.logical_and(kb <= qb, same)


def forward_kernel(span, q, kn, kc, vtn, vtc, start, attn, lse):
    i = pl.program_id(0)
    heads = q.shape[0]
    tile = q.shape[2]
    base = i * tile
    starts = start[...]
    own, below, upto = tile_masks(starts, base, tile)
    starts2 = jnp.concatenate([starts, starts], axis=1)
    queries = [q[h].reshape(2 * tile, HEAD) for h in range(heads)]
    tops, sums, accs = [], [], []
    at = pl.ds(base, tile)
    for h in range(heads):
        s0 = jnp.where(own, nt(kn[h, 0], queries[h][:tile]), NEG)
        sd = nt(kc[h, 0, at, :], queries[h])
        s1 = jnp.where(below, sd[:, :tile], NEG)
        s2 = jnp.where(upto, sd[:, tile:], NEG)
        top_n = jnp.maximum(
            jnp.max(s0, axis=0, keepdims=True), jnp.max(s1, axis=0, keepdims=True)
        )
        top_c = jnp.max(s2, axis=0, keepdims=True)
        p0 = jnp.exp(s0 - top_n)
        p1 = jnp.exp(s1 - top_n)
        p2 = jnp.exp(s2 - top_c)
        sum_n = jnp.sum(p0, axis=0, keepdims=True) + jnp.sum(p1, axis=0, keepdims=True)
        sum_c = jnp.sum(p2, axis=0, keepdims=True)
        values = vtc[h, 0, :, at]
        acc_n = nn(vtn[h, 0], p0.astype(jnp.bfloat16)) + nn(values, p1.astype(jnp.bfloat16))
        acc_c = nn(values, p2.astype(jnp.bfloat16))
        tops.append(jnp.concatenate([top_n, top_c], axis=1))
        sums.append(jnp.concatenate([sum_n, sum_c], axis=1))
        accs.append(jnp.concatenate([acc_n, acc_c], axis=1))

    def step(masked):
        def body(j, carry):
            tops, sums, accs = carry
            here = pl.ds(pl.multiple_of(j * tile, tile), tile)
            out_t, out_s, out_a = [], [], []
            for h in range(heads):
                s = nt(kc[h, 0, here, :], queries[h])
                if masked:
                    key = lax.broadcasted_iota(jnp.int32, s.shape, 0) + j * tile
                    s = jnp.where(key >= starts2, s, NEG)
                top = jnp.maximum(tops[h], jnp.max(s, axis=0, keepdims=True))
                keep = jnp.exp(tops[h] - top)
                p = jnp.exp(s - top)
                out_t.append(top)
                out_s.append(sums[h] * keep + jnp.sum(p, axis=0, keepdims=True))
                out_a.append(accs[h] * keep + nn(vtc[h, 0, :, here], p.astype(jnp.bfloat16)))
            return out_t, out_s, out_a

        return body

    carry = lax.fori_loop(span[0, i], span[1, i], step(True), (tops, sums, accs))
    tops, sums, accs = lax.fori_loop(span[1, i], i, step(False), carry)
    outs = []
    for h in range(heads):
        outs.append((accs[h] * (1.0 / sums[h])).T)
        row = tops[h] + jnp.log(sums[h])
        lse[2 * h : 2 * h + 1, :] = row[:, :tile]
        lse[2 * h + 1 : 2 * h + 2, :] = row[:, tile:]
    merged = jnp.concatenate(outs, axis=1).astype(jnp.bfloat16)
    attn[0] = merged[:tile]
    attn[1] = merged[tile:]


def unturn(values, cos, sin):
    w = values * sin
    parts = []
    for h in range(values.shape[1] // HEAD):
        lo = h * HEAD
        mid = lo + HEAD // 2
        parts += [w[:, mid : lo + HEAD], -w[:, lo:mid]]
    return values * cos + jnp.concatenate(parts, axis=1)


def backward_kernel(
    span, q, kn, kc, ktn, ktc, vn, vc, grad, attn, lse, start, masked, cosines, sines, w,
    d_all, d_a, d_spot, dk_acc, dv_acc,
):
    p = pl.program_id(0)
    i = pl.num_programs(0) - 1 - p
    heads = q.shape[0]
    tile = q.shape[2]
    base = i * tile
    at = pl.ds(base, tile)

    @pl.when(p == 0)
    def _():
        dk_acc[...] = jnp.zeros_like(dk_acc)
        dv_acc[...] = jnp.zeros_like(dv_acc)
        d_spot[...] = jnp.zeros_like(d_spot)

    starts = start[...]
    own, below, upto = tile_masks(starts, base, tile)
    starts2 = jnp.concatenate([starts, starts], axis=1)
    queries, grads, lses, deltas = [], [], [], []
    grad_n, grad_c = grad[0], grad[1]
    dots_n = grad_n.astype(jnp.float32) * attn[0].astype(jnp.float32)
    dots_c = grad_c.astype(jnp.float32) * attn[1].astype(jnp.float32)
    for h in range(heads):
        lanes = slice(h * HEAD, (h + 1) * HEAD)
        queries.append(q[h].reshape(2 * tile, HEAD))
        grads.append(jnp.concatenate([grad_n[:, lanes], grad_c[:, lanes]], axis=0))
        lses.append(
            jnp.concatenate([lse[2 * h : 2 * h + 1, :], lse[2 * h + 1 : 2 * h + 2, :]], axis=1)
        )
        dots = jnp.concatenate([dots_n[:, lanes], dots_c[:, lanes]], axis=0)
        deltas.append(jnp.sum(dots.T, axis=0, keepdims=True))

    dqs, dk_noisy, dv_noisy = [], [], []
    for h in range(heads):
        qn, gn = queries[h][:tile], grads[h][:tile]
        s0 = nt(kn[h, 0], qn)
        p0 = jnp.where(own, jnp.exp(s0 - lses[h][:, :tile]), 0.0)
        ds0 = (p0 * (nt(vn[h, 0], gn) - deltas[h][:, :tile])).astype(jnp.bfloat16)
        dv_noisy.append(nn(p0.astype(jnp.bfloat16), gn))
        dk_noisy.append(nn(ds0, qn))
        dq_n = nn(ktn[h, 0], ds0)
        both = jnp.concatenate([below, upto], axis=1)
        s = nt(kc[h, 0, at, :], queries[h])
        pr = jnp.where(both, jnp.exp(jnp.where(both, s, NEG) - lses[h]), 0.0)
        ds = (pr * (nt(vc[h, 0, at, :], grads[h]) - deltas[h])).astype(jnp.bfloat16)
        dv_acc[h, at, :] += nn(pr.astype(jnp.bfloat16), grads[h])
        dk_acc[h, at, :] += nn(ds, queries[h])
        dq = nn(ktc[h, 0, :, at], ds)
        dqs.append(dq + jnp.concatenate([dq_n, jnp.zeros_like(dq_n)], axis=1))

    def step(masked_step):
        def body(j, carry):
            out = []
            here = pl.ds(pl.multiple_of(j * tile, tile), tile)
            for h in range(heads):
                s = nt(kc[h, 0, here, :], queries[h])
                if masked_step:
                    key = lax.broadcasted_iota(jnp.int32, s.shape, 0) + j * tile
                    s = jnp.where(key >= starts2, s, NEG)
                pr = jnp.exp(s - lses[h])
                ds = (pr * (nt(vc[h, 0, here, :], grads[h]) - deltas[h])).astype(jnp.bfloat16)
                dv_acc[h, here, :] += nn(pr.astype(jnp.bfloat16), grads[h])
                dk_acc[h, here, :] += nn(ds, queries[h])
                out.append(carry[h] + nn(ktc[h, 0, :, here], ds))
            return out

        return body

    carry = lax.fori_loop(span[0, i], span[1, i], step(True), dqs)
    dqs = lax.fori_loop(span[1, i], i, step(False), carry)

    scale = 1.0 / math.sqrt(HEAD)
    dq_n = jnp.concatenate([dqs[h][:, :tile].T for h in range(heads)], axis=1) * scale
    dq_c = jnp.concatenate([dqs[h][:, tile:].T for h in range(heads)], axis=1) * scale
    dk_c = jnp.concatenate([dk_acc[h, at, :] for h in range(heads)], axis=1)
    dv_c = jnp.concatenate([dv_acc[h, at, :] for h in range(heads)], axis=1)
    dk_n = jnp.concatenate(dk_noisy, axis=1)
    dv_n = jnp.concatenate(dv_noisy, axis=1)
    hidden = masked[...].astype(jnp.float32)
    shown = 1.0 - hidden
    cos, sin = cosines[...], sines[...]
    back = jnp.zeros(d_a.shape, jnp.float32)
    for index, (noisy, clean) in enumerate(((dq_n, dq_c), (dk_n, dk_c), (dv_n, dv_c))):
        kept = clean + shown * noisy
        gone = hidden * noisy
        if index < 2:
            kept = unturn(kept, cos, sin)
            gone = unturn(gone, cos, sin)
        low = kept.astype(jnp.bfloat16)
        d_all[index] = low
        back = back + nt(low, w[index])
        d_spot[index] += jnp.sum(gone.reshape(tile // 8, 8, gone.shape[1]), axis=0)
    d_a[...] = back.astype(jnp.bfloat16)


def tile_of(shape, axis, tile, turn):
    block = tuple(tile if d == axis else s for d, s in enumerate(shape))
    return pl.BlockSpec(block, lambda i, *_: tuple(turn(i) if d == axis else 0 for d in range(len(shape))))


def whole(shape):
    return pl.BlockSpec(shape, lambda i, *_: (0,) * len(shape))


def half(shape, copy, axis, tile, turn):
    block = tuple(1 if d == 1 else tile if d == axis else s for d, s in enumerate(shape))
    return pl.BlockSpec(
        block, lambda i, *_: tuple(copy if d == 1 else turn(i) if d == axis else 0 for d in range(len(shape)))
    )


def project(a, amask, masked, w, wrot, cosines, sines):
    group, width = a.shape
    lw = w.shape[2]
    heads = lw // HEAD
    tile = min(TILE, group)
    same = lambda i: i
    flat = (heads, 2, group, HEAD)
    trans = (heads, 2, HEAD, group)
    bf = jnp.bfloat16
    return pl.pallas_call(
        project_kernel,
        grid=(group // tile,),
        in_specs=[
            tile_of((group, width), 0, tile, same),
            whole(amask.shape),
            tile_of((group, 1), 0, tile, same),
            whole(w.shape),
            whole(wrot.shape),
            tile_of((group, lw), 0, tile, same),
            tile_of((group, lw), 0, tile, same),
        ],
        out_specs=[
            tile_of(flat, 2, tile, same),
            tile_of(flat, 2, tile, same),
            tile_of(trans, 3, tile, same),
            tile_of(flat, 2, tile, same),
            tile_of(trans, 3, tile, same),
        ],
        out_shape=[jax.ShapeDtypeStruct(s, bf) for s in (flat, flat, trans, flat, trans)],
        name="project",
    )(a, amask, masked, w, wrot, cosines, sines)


def attend(span, q, k, v_t, start):
    heads, _, group, _ = q.shape
    tile = min(TILE, group)
    same = lambda i: i
    lw = heads * HEAD
    return pl.pallas_call(
        forward_kernel,
        grid_spec=pltpu.PrefetchScalarGridSpec(
            num_scalar_prefetch=1,
            grid=(group // tile,),
            in_specs=[
                tile_of(q.shape, 2, tile, same),
                half(k.shape, 0, 2, tile, same),
                half(k.shape, 1, None, tile, same),
                half(v_t.shape, 0, 3, tile, same),
                half(v_t.shape, 1, None, tile, same),
                tile_of((1, group), 1, tile, same),
            ],
            out_specs=[
                tile_of((2, group, lw), 1, tile, same),
                tile_of((8, group), 1, tile, same),
            ],
        ),
        out_shape=[
            jax.ShapeDtypeStruct((2, group, lw), jnp.bfloat16),
            jax.ShapeDtypeStruct((8, group), jnp.float32),
        ],
        name="attend",
    )(span, q, k, k, v_t, v_t, start)


def attend_back(span, q, k, k_t, v, grad, attn, lse, start, masked, cosines, sines, w):
    heads, _, group, _ = q.shape
    tile = min(TILE, group)
    lw = heads * HEAD
    width = w.shape[1]
    last = group // tile - 1
    turn = lambda i: last - i
    return pl.pallas_call(
        backward_kernel,
        grid_spec=pltpu.PrefetchScalarGridSpec(
            num_scalar_prefetch=1,
            grid=(group // tile,),
            in_specs=[
                tile_of(q.shape, 2, tile, turn),
                half(k.shape, 0, 2, tile, turn),
                half(k.shape, 1, None, tile, turn),
                half(k_t.shape, 0, 3, tile, turn),
                half(k_t.shape, 1, None, tile, turn),
                half(v.shape, 0, 2, tile, turn),
                half(v.shape, 1, None, tile, turn),
                tile_of((2, group, lw), 1, tile, turn),
                tile_of((2, group, lw), 1, tile, turn),
                tile_of((8, group), 1, tile, turn),
                tile_of((1, group), 1, tile, turn),
                tile_of((group, 1), 0, tile, turn),
                tile_of((group, lw), 0, tile, turn),
                tile_of((group, lw), 0, tile, turn),
                whole(w.shape),
            ],
            out_specs=[
                tile_of((3, group, lw), 1, tile, turn),
                tile_of((group, width), 0, tile, turn),
                whole((3, 8, lw)),
            ],
            scratch_shapes=[
                pltpu.VMEM((heads, group, HEAD), jnp.float32),
                pltpu.VMEM((heads, group, HEAD), jnp.float32),
            ],
        ),
        out_shape=[
            jax.ShapeDtypeStruct((3, group, lw), jnp.bfloat16),
            jax.ShapeDtypeStruct((group, width), jnp.bfloat16),
            jax.ShapeDtypeStruct((3, 8, lw), jnp.float32),
        ],
        name="attend_back",
    )(span, q, k, k, k_t, k_t, v, v, grad, attn, lse, start, masked, cosines, sines, w)


def layer_norm(values, gain, shift):
    center = values - jnp.mean(values, axis=-1, keepdims=True)
    spread = jnp.mean(center * center, axis=-1, keepdims=True)
    return center * lax.rsqrt(spread + EPS) * gain + shift


def gelu_tanh(values):
    return jax.nn.gelu(values, approximate=True)


def token_meta(lengths_row, count):
    ends = jnp.cumsum(lengths_row)
    starts = ends - lengths_row
    places = jnp.arange(count)
    seq_id = jnp.sum((places[:, None] >= ends[None, :]).astype(jnp.int32), axis=1)
    slot_ids = jnp.arange(lengths_row.shape[0])
    first = jnp.sum(jnp.where(seq_id[:, None] == slot_ids[None, :], starts[None, :], 0), axis=1)
    return (first, places - first)


def angle_tables(positions, heads):
    index_f = jnp.arange(HEAD // 2).astype(jnp.float32)
    freqs = jnp.exp(index_f * (-2.0 * math.log(10000.0) / HEAD))
    angles = positions.astype(jnp.float32)[:, None] * freqs[None, :]
    return (jnp.tile(jnp.cos(angles), (1, 2 * heads)), jnp.tile(jnp.sin(angles), (1, 2 * heads)))


def total(value):
    for name in ("narrow", "wide"):
        size = lax.axis_size(name)
        if size & (size - 1):
            value = lax.psum(value, name)
            continue
        step = 1
        while step < size:
            value = value + lax.ppermute(value, name, [(d, d ^ step) for d in range(size)])
            step *= 2
    return value


def einsum(spec, left, right):
    return jnp.einsum(spec, left, right, preferred_element_type=jnp.float32)


def per_device(
    tokens,
    noise,
    seq_lengths,
    ln1_gain,
    ln1_bias,
    qkv_weight,
    out_weight,
    ln2_gain,
    ln2_bias,
    up_weight,
    up_bias,
    down_weight,
    down_bias,
    mask_vector,
    cotangent,
):
    f32 = jnp.float32
    bf16 = jnp.bfloat16
    both = ("narrow", "wide")
    ways = lax.axis_size("wide")
    parts = lax.axis_size("narrow")
    lane = lax.axis_index("wide")
    rows, width = tokens.shape
    group = rows * parts
    lw = qkv_weight.shape[2]
    ff = up_weight.shape[1]
    heads = lw // HEAD

    clean = tokens.astype(f32)
    normed1, norm1_pull = jax.vjp(layer_norm, clean, ln1_gain, ln1_bias)
    spot = mask_vector[None, :]
    normed_m, norm_m_pull = jax.vjp(layer_norm, spot, ln1_gain, ln1_bias)
    a_all = lax.all_gather(normed1.astype(bf16), "narrow", axis=0, tiled=True)
    noise_all = lax.all_gather(noise, "narrow", axis=0, tiled=True)
    spot_row = jnp.broadcast_to(normed_m.astype(bf16), (16, width))

    def share(weight):
        step = weight.shape[0] // ways
        return lax.dynamic_slice_in_dim(weight, lane * step, step, 0)

    a_all, up_s, down_s, out_s, bias_s = lax.optimization_barrier(
        (a_all, share(up_weight), share(down_weight), share(out_weight), up_bias)
    )
    out_full = lax.all_gather(out_s, both, axis=0, tiled=True)
    up_full = lax.all_gather(up_s, both, axis=0, tiled=True).reshape(parts, width, ff)
    down_full = lax.all_gather(down_s, both, axis=0, tiled=True).reshape(parts, ff, width)
    bias_full = lax.all_gather(bias_s, "narrow", axis=0)

    first, pos = token_meta(seq_lengths[0], group)
    cosines, sines = angle_tables(pos, heads)
    start = first[None, :].astype(jnp.int32)
    tile = min(TILE, group)
    tiles = group // tile
    at_head = first[::tile] // tile
    at_tail = (first[tile - 1 :: tile] + (tile - 1)) // tile
    span = jnp.stack([at_head, jnp.minimum(at_tail, jnp.arange(tiles))]).astype(jnp.int32)
    halves = qkv_weight[:2].reshape(2, width, heads, 2, HEAD // 2)
    wrot = jnp.stack([-halves[:, :, :, 1], halves[:, :, :, 0]], axis=3).reshape(2, width, lw)
    masked_all = noise_all[:, None]

    q, k, k_t, v, v_t = project(a_all, spot_row, masked_all, qkv_weight, wrot, cosines, sines)
    attn, lse = attend(span, q, k, v_t, start)

    sent = attn.reshape(2, parts, rows, lw)
    attn_rows = lax.all_to_all(sent, "narrow", 1, 1)
    attn_rows = attn_rows.transpose(0, 2, 1, 3).reshape(2, rows, width)
    masked = noise[:, None] == 1
    noisy = jnp.where(masked, spot, clean)
    resid = jnp.stack([noisy, clean])
    h_mid = resid + einsum("ctd,de->cte", attn_rows, out_full)
    normed2, norm2_pull = jax.vjp(layer_norm, h_mid, ln2_gain, ln2_bias)
    b = normed2.astype(bf16).reshape(2 * rows, width)
    up_pre = einsum("td,ndf->ntf", b, up_full) + bias_full[:, None, :]
    hidden_f, gelu_pull = jax.vjp(gelu_tanh, up_pre)
    hidden = hidden_f.astype(bf16)
    mlp_out = einsum("ntf,nfd->td", hidden, down_full).reshape(2, rows, width)
    output = (h_mid + mlp_out + down_bias).astype(bf16)

    cot = cotangent.reshape(2 * rows, width)
    grad_out = cotangent.astype(f32)
    d_down_bias = jnp.sum(grad_out, axis=(0, 1))
    d_hidden = einsum("td,nfd->ntf", cot, down_full)
    d_up_low = gelu_pull(d_hidden)[0].astype(bf16)
    d_b = einsum("ntf,ndf->td", d_up_low, up_full).reshape(2, rows, width)
    d_h_ln, d_ln2_gain, d_ln2_bias = norm2_pull(d_b)
    d_h_mid = grad_out + d_h_ln
    d_z = d_h_mid.astype(bf16)
    d_attn = einsum("cte,de->ctd", d_z, out_full).astype(bf16)
    d_attn = d_attn.reshape(2, rows, parts, lw).transpose(0, 2, 1, 3)
    d_attn = lax.all_to_all(d_attn, "narrow", 1, 1).reshape(2, group, lw)

    d_down = einsum("td,ntf->ndf", cot, hidden)
    d_up = einsum("td,ntf->ndf", b, d_up_low)
    d_up_bias = jnp.sum(d_up_low, axis=1, dtype=f32)
    d_out = einsum("cte,ctd->ed", d_z, attn_rows)
    d_out = d_out.reshape(width, parts, lw).transpose(1, 0, 2)

    def scatter(value):
        return lax.psum_scatter(
            value.astype(bf16).reshape(-1, value.shape[-1]), both, scatter_dimension=0, tiled=True
        ).astype(f32)

    d_down_mine = scatter(d_down).T
    d_up_mine = scatter(d_up)
    d_out_mine = scatter(d_out).T
    early = total(
        jnp.concatenate([d_ln2_gain, d_ln2_bias, d_down_bias, d_up_bias.reshape(-1)])
    )

    d_all, d_a_part, d_spot = attend_back(
        span, q, k, k_t, v, d_attn, attn, lse, start, masked_all, cosines, sines, qkv_weight
    )
    d_a = lax.psum_scatter(d_a_part, "narrow", scatter_dimension=0, tiled=True).astype(f32)
    d_spot = jnp.sum(d_spot, axis=1)
    d_qkv = einsum("td,xte->xde", a_all, d_all) + (
        spot_row[0].astype(f32)[None, :, None] * d_spot[:, None, :]
    )
    d_qkv = lax.psum_scatter(d_qkv.astype(bf16), "wide", scatter_dimension=1, tiled=True).astype(f32)
    d_a_spot = jnp.einsum(
        "xe,xde->d", d_spot, qkv_weight.astype(f32), precision=lax.Precision.HIGHEST
    )
    d_h_spot = jnp.sum(jnp.where(masked, d_h_mid[0], 0.0), axis=0)
    d_row, d_ln1_gain, d_ln1_bias = norm1_pull(d_a)
    d_tokens = (d_h_mid[1] + jnp.where(masked, 0.0, d_h_mid[0]) + d_row).astype(bf16)
    late = total(jnp.concatenate([d_ln1_gain, d_ln1_bias, d_h_spot, d_a_spot]))
    d_ln1_gain, d_ln1_bias, d_h_spot, d_a_spot = late.reshape(4, width)
    d_mask, gain_m, bias_m = norm_m_pull(d_a_spot[None, :])
    d_ln2_gain, d_ln2_bias, d_down_bias = early[: 3 * width].reshape(3, width)
    step = ff // ways
    mine = (lax.axis_index("narrow") * ways + lane) * step
    return (
        output,
        d_tokens,
        d_ln1_gain + gain_m,
        d_ln1_bias + bias_m,
        d_qkv,
        d_out_mine,
        d_ln2_gain,
        d_ln2_bias,
        d_up_mine,
        lax.dynamic_slice_in_dim(early[3 * width :], mine, step, 0),
        d_down_mine,
        d_down_bias,
        d_h_spot + d_mask[0],
    )


def solution(mesh):
    placed = (
        P(("wide", "narrow"), None),
        P(("wide", "narrow")),
        P("wide", None),
        P(),
        P(),
        P(None, None, "narrow"),
        P("narrow", None),
        P(),
        P(),
        P(None, "narrow"),
        P("narrow"),
        P("narrow", None),
        P(),
        P(),
        P(None, ("wide", "narrow"), None),
    )
    return jax.shard_map(
        per_device,
        mesh=mesh,
        in_specs=placed,
        out_specs=(
            P(None, ("wide", "narrow"), None),
            P(("wide", "narrow"), None),
            P(),
            P(),
            P(None, "wide", "narrow"),
            P("narrow", "wide"),
            P(),
            P(),
            P("wide", "narrow"),
            P(("narrow", "wide")),
            P("narrow", "wide"),
            P(),
            P(),
        ),
        check_vma=False,
    )
```

time: 2380 us -> 892 us (0.37)
  matrix products: 833 us -> 87.2 us
  waiting for transfers between devices: 918 us -> 481 us
  other arithmetic: 427 us -> 55.8 us
  local copies, waits for them, and re-layouts: 130 us -> 41.2 us
  Pallas kernels: 0 us -> 85.7 us
  blocking collectives: 41.5 us -> 98.3 us
    dot_general x73 -> x11, matrix products: 830 us -> 87.2 us  [the longest x10 85.5 us: einsum(): return jnp.einsum(spec, left, right, preferred_element_type=jnp.float32)]
    all_gather x4, waiting for transfers between devices: 444 us -> 124 us  [the longest x1 63.9 us: per_device(): a_all = lax.all_gather(normed1.astype(bf16), 'narrow', axis=0, tiled=True)]
    reduce_scatter x6 -> x3, waiting for transfers between devices: 473 us -> 234 us  [the longest x2 220 us: scatter(): lax.psum_scatter(value.astype(bf16).reshape(-1, value.shape[-1]), both, s...]
    convert_element_type x14 -> x4, other arithmetic: 189 us -> 6.34 us  [the longest x1 3 us: per_device(): a_all = lax.all_gather(normed1.astype(bf16), 'narrow', axis=0, tiled=True)]
    unnamed x16 -> x11, waiting for transfers between devices: 0.75 us -> 110 us
    pallas_call x0 -> x3, Pallas kernels: none -> 85.7 us  [the longest x1 42.2 us: attend_back(): pl.pallas_call(backward_kernel, grid_spec=pltpu.PrefetchScalarGridSpec(nu...]
    and x16 -> x0, other arithmetic: 84.8 us -> none  [allowed_pairs(): return jnp.logical_and(same, rule)]
    reduce_sum x9 -> x4, other arithmetic: 96.7 us -> 18.1 us  [the longest x1 13.6 us: per_device(): d_up_bias = jnp.sum(d_up_low, axis=1, dtype=f32)]
  transfers between devices with their start and end apart: 13 -> 20, of which waited for: 9 -> 11; matrix products, arithmetic and copies ran while one was open for 41% -> 13% of each run, Pallas kernels for 0% -> 5%
where the time goes in v1:
time: 892 us; the launch traced here: 885 us
  waiting for transfers between devices  481 us (54%)
  blocking collectives  98.3 us (11%)
  matrix products  87.2 us (10%)
  Pallas kernels  85.7 us (10%)
  other arithmetic  55.8 us (6%)
  local copies, waits for them, and re-layouts  41.2 us (5%)
  starting transfers between devices  18.8 us (2%)
  between operations  17.5 us (2%)
    reduce_scatter x2, waiting for transfers between devices, scatter(): lax.psum_scatter(value.astype(bf16).reshape(-1, value.shape[-1]), both, s...  220 us
    unnamed x11, waiting for transfers between devices  110 us
    dot_general x10, matrix products, einsum(): return jnp.einsum(spec, left, right, preferred_element_type=jnp.float32)  85.5 us
    all_gather x1, waiting for transfers between devices, per_device(): a_all = lax.all_gather(normed1.astype(bf16), 'narrow', axis=0, tiled=True)  63.9 us
    all_gather x1, waiting for transfers between devices, per_device(): lax.all_gather(down_s, both, axis=0, tiled=True).reshape(parts, ff, width)  56.3 us
    all_gather x1, blocking collectives, per_device(): bias_full = lax.all_gather(bias_s, 'narrow', axis=0)  45.5 us
    pallas_call x1, Pallas kernels, attend_back(): pl.pallas_call(backward_kernel, grid_spec=pltpu.PrefetchScalarGridSpec(nu...  42.2 us
    all_to_all x1, blocking collectives, per_device(): d_attn = lax.all_to_all(d_attn, 'narrow', 1, 1).reshape(2, group, lw)  40.8 us
  transfers between devices with their start and end apart: 20, of which 11 were waited for; matrix products, arithmetic and copies ran while one was open for 13% of the time, Pallas kernels for 5%

profile of v1, /device:TPU:0, one launch (start us, length us, event | category | flops | bytes accessed | tf_op | source)
XLA Modules:
  0.0 885.0 jit_solution(5244023146599913558)
XLA Ops:
  16.3 63.9 %all-gather.8.cloned.1.call-done.a = bf16[2048,768]{1,0:T(8,128)(2,1)} async-done(((bf16[512,768]{1,0:T(8,128)(2,1)}), bf16[2048,768]{1,0:T(8,128)(2,1)}) %all-gather.8.cloned.1.call-update) | async-done | bytes 3145744 | tf_op jit(solution)/shard_map/all_gather | solution.py:449
  86.2 11.9 %all-gather.1 = s32[4,1,512]{2,1,0:T(1,128)S(1)} all-gather(s32[1,1,512]{2,1,0:T(1,128)S(1)} %bitcast.247), channel_id=1, replica_groups=mesh['wide'=8,'narrow'=4] {'narrow'}, dimensions={0}, use_global_device_ids=true | all-gather | bytes 10240 | tf_op jit(solution)/shard_map/all_gather | solution.py:450
  107.0 15.9 %project.1 = (bf16[3,2,2048,64]{3,2,1,0:T(8,128)(2,1)}, bf16[3,2,2048,64]{3,2,1,0:T(8,128)(2,1)}, bf16[3,2,64,2048]{3,2,1,0:T(8,128)(2,1)}, bf16[3,2,2048,64]{3,2,1,0:T(8,128)(2,1)}, bf16[3,2,64,2048]{3,2,1,0:T(8,128)(2,1)}) custom-call(bf16[2048,768]{1,0:T(8,128)(2,1)} %all-gather.8.cloned.1.call-done.a, bf16[16,768]{1,0:T(8,128)(2,1)} %broadcast_in_dim.73.amask, ...), custom_call_target="tpu_custom_call" | custom-call | tf_op jit(solution)/shard_map/project/pallas_call | solution.py:269
  122.8 27.6 %attend.1 = (bf16[2,2048,192]{2,1,0:T(8,128)(2,1)}, f32[8,2048]{1,0:T(8,128)}) custom-call(s32[2,8]{1,0:T(2,128)} %pad_add_fusion.span, bf16[3,2,2048,64]{3,2,1,0:T(8,128)(2,1)} %get-tuple-element.29.q, bf16[3,2,2048,64]{3,2,1,0:T(8,128)(2,1)} %get-tuple-element.30.kn.kc, bf16[3,2,2048,64]{3,2,1,0:T(8,128)(2,1)} %get-tuple-element.30.kn.kc, ...), custom_call_target="tpu_custom_call" | custom-call | tf_op jit(solution)/shard_map/attend/pallas_call | solution.py:298
  159.6 45.5 %all-gather.2 = f32[4,1,768]{2,1,0:T(1,128)S(1)} all-gather(f32[1,1,768]{2,1,0:T(1,128)S(1)} %reshape.322), channel_id=2, replica_groups=mesh['wide'=8,'narrow'=4] {'narrow'}, dimensions={0}, use_global_device_ids=true | all-gather | bytes 15360 | tf_op jit(solution)/shard_map/all_gather | solution.py:463
  217.4 10.6 %fusion.85 = f32[4,768,1024]{2,1,0:T(8,128)} fusion(bf16[4,768,768]{2,1,0:T(8,128)(2,1)} %bitcast.251, bf16[1024,768,1]{1,0,2:T(8,128)(2,1)} %bitcast.237), kind=kOutput, calls=%fused_computation.159 | convolution fusion | flops 4831838208 | bytes 18874368 | tf_op jit(solution)/shard_map/td,ndf->ntf/dot_general | solution.py:413
  228.0 56.3 %all-gather.14.cloned.1.call-done = bf16[3072,768]{1,0:T(8,128)(2,1)} async-done(((bf16[96,768]{1,0:T(8,128)(2,1)}), bf16[3072,768]{1,0:T(8,128)(2,1)}) %all-gather.14.cloned.1.call-update) | async-done | bytes 4718608 | tf_op jit(solution)/shard_map/all_gather | solution.py:462
  284.4 21.7 %fusion.6 = (bf16[1024,768,4]{0,1,2:T(8,128)(2,1)}, bf16[1024,768,4]{0,1,2:T(8,128)(2,1)}, f32[4,768,1024]{2,1,0:T(8,128)}) fusion(f32[4,768,1024]{2,1,0:T(8,128)} %fusion.85, f32[768,4]{0,1:T(4,128)S(1)} %bitcast.242, bf16[4,768,768]{2,1,0:T(8,128)(2,1)} %bitcast.249, bf16[1024,768,1]{1,0,2:T(8,128)(2,1)} %bitcast.234), kind=kOutput, calls=%fused_computation.10 | convolution fusion | flops 4904189952 | bytes 44052480 | tf_op jit(solution)/shard_map/td,nfd->ntf/dot_general | solution.py:413
  306.1 7.6 multiply_reduce_fusion
  313.7 13.6 %fusion.31 = (f32[768]{0:T(1024)S(1)}, f32[2,512]{1,0:T(2,128)S(1)}, f32[768]{0:T(1024)S(1)}) fusion(f32[2,512,768,1]{2,1,3,0:T(8,128)S(1)} %get-tuple-element.131, f32[2,512,768]{2,1,0:T(8,128)S(1)} %get-tuple-element.128, f32[2,512]{1,0:T(2,128)S(1)} %fusion.71, f32[2,512]{1,0:T(2,128)S(1)} %broadcast_multiply_fusion, ...), kind=kLoop, calls=%fused_computation.49 | loop fusion | flops 8648192 | bytes 6317056 | tf_op jit(solution)/shard_map/transpose(jvp())/reduce_sum | solution.py:375
  337.0 40.8 %all_to_all.10 = bf16[2,4,512,192]{2,3,0,1:T(8,128)(2,1)} all-to-all(bf16[2,4,512,192]{2,3,0,1:T(8,128)(2,1)S(1)} %copy.106), channel_id=1, replica_groups=mesh['wide'=8,'narrow'=4] {'narrow'}, dimensions={1} | all-to-all | bytes 3145728 | tf_op jit(solution)/shard_map/all_to_all | solution.py:506
  381.9 42.2 %attend_back.1 = (bf16[3,2048,192]{2,1,0:T(8,128)(2,1)}, bf16[2048,768]{1,0:T(8,128)(2,1)}, f32[3,8,192]{2,1,0:T(8,128)}) custom-call(s32[2,8]{1,0:T(2,128)} %pad_add_fusion.span, bf16[3,2,2048,64]{3,2,1,0:T(8,128)(2,1)} %get-tuple-element.29.q, bf16[3,2,2048,64]{3,2,1,0:T(8,128)(2,1)} %get-tuple-element.30.kn.kc, ...), custom_call_target="tpu_custom_call" | custom-call | tf_op jit(solution)/shard_map/attend_back/pallas_call | solution.py:331
  431.7 5.9 fusion.45
  445.2 11.4 %fusion.34 = bf16[4,768,768]{1,2,0:T(8,128)(2,1)} fusion(bf16[1024,768,1]{1,0,2:T(8,128)(2,1)} %bitcast.235, f32[4,768,1024]{2,1,0:T(8,128)} %fusion.85, f32[4,768]{1,0:T(4,128)S(1)} %bitcast.243), kind=kOutput, calls=%fused_computation.56 | convolution fusion | flops 4865654784 | bytes 18886656 | tf_op jit(solution)/shard_map/td,ntf->ndf/dot_general | solution.py:413
  456.9 13.6 %convert_reduce_fusion = (f32[4,768]{1,0:T(4,128)S(1)}, bf16[4,1024,768]{1,2,0:T(8,128)(2,1)S(1)}) fusion(f32[4,768,1024]{2,1,0:T(8,128)} %fusion.85, f32[4,768]{1,0:T(4,128)S(1)} %bitcast.244, f32[4,768,1024]{2,1,0:T(8,128)} %get-tuple-element.129), kind=kLoop, calls=%fused_computation.31 | loop fusion | flops 72348672 | bytes 31481856 | tf_op jit(solution)/shard_map/reduce_sum | solution.py:510
  470.6 6.9 convolution_convert_fusion
  477.8 6.0 collective-permute-done.5
  492.9 13.6 %reduce-scatter.10.cloned.1.call-done = bf16[512,768]{1,0:T(8,128)(2,1)} async-done(((bf16[2048,768]{1,0:T(8,128)(2,1)}), bf16[512,768]{1,0:T(8,128)(2,1)}) %reduce-scatter.10.cloned.1.call-update) | async-done | bytes 786448 | tf_op jit(solution)/shard_map/reduce_scatter | solution.py:529
  515.0 7.8 collective-permute-start.9
  524.4 9.6 %fusion.33 = bf16[2,512,768]{2,1,0:T(8,128)(2,1)} fusion(f32[2,512,768]{2,1,0:T(8,128)S(1)} %get-tuple-element.128, bf16[4,768,768,1]{2,1,0,3:T(8,128)(2,1)} %bitcast.250, bf16[4,96,2,8,512]{4,3,2,1,0:T(8,128)(2,1)} %bitcast.254, f32[768]{0:T(1024)S(1)} %copy-done.21), kind=kOutput, calls=%fused_computation.52 | convolution fusion | flops 4834197504 | bytes 15731712 | tf_op jit(solution)/shard_map/ntf,nfd->td/dot_general | solution.py:413
  535.4 73.7 %reduce-scatter.18.cloned.1.call-done = bf16[96,192]{1,0:T(8,128)(2,1)} async-done(((bf16[3072,192]{1,0:T(8,128)(2,1)}), bf16[96,192]{1,0:T(8,128)(2,1)}) %reduce-scatter.18.cloned.1.call-update) | async-done | bytes 36880
  612.2 34.9 %reduce-scatter.16.cloned.1.call-done = bf16[96,576]{1,0:T(8,128)(2,1)} async-done(((bf16[768,576]{1,0:T(8,128)(2,1)}), bf16[96,576]{1,0:T(8,128)(2,1)}) %reduce-scatter.16.cloned.1.call-update) | async-done | bytes 110608
  650.7 109.7 %reduce-scatter.14.cloned.1.call-done = bf16[96,768]{1,0:T(8,128)(2,1)} async-done(((bf16[3072,768]{1,0:T(8,128)(2,1)}), bf16[96,768]{1,0:T(8,128)(2,1)}) %reduce-scatter.14.cloned.1.call-update) | async-done | bytes 147472 | tf_op jit(solution)/shard_map/reduce_scatter | solution.py:515
  762.0 110.6 %reduce-scatter.12.cloned.1.call-done = bf16[96,768]{1,0:T(8,128)(2,1)} async-done(((bf16[3072,768]{1,0:T(8,128)(2,1)}), bf16[96,768]{1,0:T(8,128)(2,1)}) %reduce-scatter.12.cloned.1.call-update) | async-done | bytes 147472 | tf_op jit(solution)/shard_map/reduce_scatter | solution.py:515
  (174 shorter events, 105.9 us)
Async XLA Ops:
  7.2 74.4 %copy-start.22 = (s32[1,4]{1,0:T(1,128)S(1)}, s32[1,4]{1,0:T(1,128)}, u32[]{:S(2)}) copy-start(s32[1,4]{1,0:T(1,128)} %param.17) | copy-start | bytes 52
  7.2 74.9 %copy-start.7 = (bf16[3,768,192]{1,2,0:T(8,128)(2,1)S(1)}, bf16[3,768,192]{1,2,0:T(8,128)(2,1)}, u32[]{:S(2)}) copy-start(bf16[3,768,192]{1,2,0:T(8,128)(2,1)} %param.20) | copy-start | bytes 2654212
  7.2 73.0 %all-gather.8.cloned.1.call-start = ((), (), s32[]{:S(2)}) async-start(), calls=%async_computation.7 | async-start | bytes 3932160 | tf_op jit(solution)/shard_map/all_gather | solution.py:449
  13.9 85.6 %slice-start = ((bf16[3,768,192]{1,2,0:T(8,128)(2,1)}), bf16[2,768,192]{1,2,0:T(8,128)(2,1)S(1)}, s32[]{:S(2)}) async-start(bf16[3,768,192]{1,2,0:T(8,128)(2,1)} %param.20), calls=%async_computation.16 | async-start | bytes 1179648 | tf_op jit(solution)/shard_map/slice | solution.py:473
  13.9 192.6 %all-gather.10.cloned.1.call-start = ((), (), s32[]{:S(2)}) async-start(), calls=%async_computation.8 | async-start | bytes 1216512 | tf_op jit(solution)/shard_map/all_gather | solution.py:460
  80.2 137.1 %all-gather.12.cloned.1.call-start = ((), (), s32[]{:S(2)}) async-start(), calls=%async_computation.9 | async-start | bytes 4866048 | tf_op jit(solution)/shard_map/all_gather | solution.py:461
  81.0 203.4 %all-gather.14.cloned.1.call-start = ((), (), s32[]{:S(2)}) async-start(), calls=%async_computation.10 | async-start | bytes 4866048 | tf_op jit(solution)/shard_map/all_gather | solution.py:462
  154.5 50.5 %all-to-all-start = ((bf16[2,4,512,192]{2,3,0,1:T(8,128)(2,1)}), bf16[2,4,512,192]{2,3,0,1:T(8,128)(2,1)S(1)}, u32[]{:S(2)}, u32[]{:S(2)}) async-start(bf16[2,4,512,192]{2,3,0,1:T(8,128)(2,1)} %copy.99), calls=%async_computation | async-start | bytes 3145728 | tf_op jit(solution)/shard_map/all_to_all | solution.py:481
  158.2 348.3 %reduce-scatter.10.cloned.1.call-start = ((), (), s32[]{:S(2)}) async-start(), calls=%async_computation.11 | async-start | bytes 3932160 | tf_op jit(solution)/shard_map/reduce_scatter | solution.py:529
  424.1 185.0 %reduce-scatter.18.cloned.1.call-start = ((), (), s32[]{:S(2)}) async-start(), calls=%async_computation.15 | async-start | bytes 1622016
  431.6 215.5 %reduce-scatter.16.cloned.1.call-start = ((), (), s32[]{:S(2)}) async-start(), calls=%async_computation.14 | async-start | bytes 1105920
  445.1 315.2 %reduce-scatter.14.cloned.1.call-start = ((), (), s32[]{:S(2)}) async-start(), calls=%async_computation.13 | async-start | bytes 4866048 | tf_op jit(solution)/shard_map/reduce_scatter | solution.py:515
  456.6 415.9 %reduce-scatter.12.cloned.1.call-start = ((), (), s32[]{:S(2)}) async-start(), calls=%async_computation.12 | async-start | bytes 4866048 | tf_op jit(solution)/shard_map/reduce_scatter | solution.py:515
  477.5 6.3 collective-permute-start.5
  483.9 5.4 collective-permute-start.6
  489.3 1.2 collective-permute-start.7
  490.5 24.5 %collective-permute-start.8 = (f32[5376]{0:T(1024)S(1)}, f32[5376]{0:T(1024)S(1)}, u32[]{:S(2)}, u32[]{:S(2)}) collective-permute-start(f32[5376]{0:T(1024)S(1)} %add.220), channel_id=1, source_target_pairs={{0,8},{4,12},{8,0},{12,4},{16,24},{20,28},{24,16},{28,20},{1,9},{5... | collective-permute-start | bytes 64520 | tf_op jit(solution)/shard_map/ppermute | solution.py:407
  514.0 8.9 %collective-permute-start = (f32[3072]{0:T(1024)S(1)}, f32[3072]{0:T(1024)S(1)}, u32[]{:S(2)}, u32[]{:S(2)}) collective-permute-start(f32[3072]{0:T(1024)S(1)} %pad_maximum_fusion.2), channel_id=1, source_target_pairs={{0,1},{1,0},{2,3},{3,2},{4,5},{5,4},{6,7},{7,6},{8,9},{9,8},{10,11... | collective-permute-start | bytes 36872 | tf_op jit(solution)/shard_map/ppermute | solution.py:407
  515.0 19.1 %collective-permute-start.9 = (f32[5376]{0:T(1024)S(1)}, f32[5376]{0:T(1024)S(1)}, u32[]{:S(2)}, u32[]{:S(2)}) collective-permute-start(f32[5376]{0:T(1024)S(1)} %add.221), channel_id=1, source_target_pairs={{0,16},{4,20},{8,24},{12,28},{16,0},{20,4},{24,8},{28,12},{1,17},{... | collective-permute-start | bytes 64520 | tf_op jit(solution)/shard_map/ppermute | solution.py:407
  522.9 11.2 %collective-permute-start.1 = (f32[3072]{0:T(1024)S(1)}, f32[3072]{0:T(1024)S(1)}, u32[]{:S(2)}, u32[]{:S(2)}) collective-permute-start(f32[3072]{0:T(1024)S(1)} %fusion.98), channel_id=1, source_target_pairs={{0,2},{1,3},{2,0},{3,1},{4,6},{5,7},{6,4},{7,5},{8,10},{9,11},{10,... | collective-permute-start | bytes 36872 | tf_op jit(solution)/shard_map/ppermute | solution.py:407
  524.4 353.6 %copy-start.1 = (bf16[192,768]{1,0:T(8,128)(2,1)S(1)}, bf16[192,768]{1,0:T(8,128)(2,1)}, u32[]{:S(2)}) copy-start(bf16[192,768]{1,0:T(8,128)(2,1)} %param.21) | copy-start | bytes 884740
  534.1 75.9 %collective-permute-start.2 = (f32[3072]{0:T(1024)S(1)}, f32[3072]{0:T(1024)S(1)}, u32[]{:S(2)}, u32[]{:S(2)}) collective-permute-start(f32[3072]{0:T(1024)S(1)} %add.206), channel_id=1, source_target_pairs={{0,4},{4,0},{8,12},{12,8},{16,20},{20,16},{24,28},{28,24},{1,5},{5... | collective-permute-start | bytes 36872 | tf_op jit(solution)/shard_map/ppermute | solution.py:407
  610.0 39.1 %collective-permute-start.3 = (f32[3072]{0:T(1024)S(1)}, f32[3072]{0:T(1024)S(1)}, u32[]{:S(2)}, u32[]{:S(2)}) collective-permute-start(f32[3072]{0:T(1024)S(1)} %add.207), channel_id=1, source_target_pairs={{0,8},{4,12},{8,0},{12,4},{16,24},{20,28},{24,16},{28,20},{1,9},{5... | collective-permute-start | bytes 36872 | tf_op jit(solution)/shard_map/ppermute | solution.py:407
  649.2 225.0 %collective-permute-start.4 = (f32[3072]{0:T(1024)S(1)}, f32[3072]{0:T(1024)S(1)}, u32[]{:S(2)}, u32[]{:S(2)}) collective-permute-start(f32[3072]{0:T(1024)S(1)} %add.208), channel_id=1, source_target_pairs={{0,16},{4,20},{8,24},{12,28},{16,0},{20,4},{24,8},{28,12},{1,17},{... | collective-permute-start | bytes 36872 | tf_op jit(solution)/shard_map/ppermute | solution.py:407
  (20 other events, 267.1 us)
Sparse Core Ops, SparseCore 0:
  14.0 66.1 all-gather.7
  83.7 52.5 all-gather.9
  139.7 77.5 all-gather.11
  220.7 63.6 all-gather.13
  424.3 82.2 reduce-scatter.9
  511.6 97.4 reduce-scatter.17
  612.3 34.7 reduce-scatter.15
  652.6 107.7 reduce-scatter.13
  765.8 106.6 reduce-scatter.11
